TPU v7x, 32 devices: a whole 2x2x4 slice. The times are simulated.
32 devices in a mesh: doc: 4 (over z), feat: 8 (over y, x, core).
Axes of the slice: x: 2, y: 2, z: 4, core: 2. Of those that a mesh axis runs over, the one named last changes fastest.
Arguments:
- documents: bfloat16 [512, 512], P('doc', 'feat'), may hold values from -6 to 6
- directions: bfloat16 [512, 32768], P('doc', 'feat'), may hold values from -0.5 to 0.5
- phase: float32 [32768], P('feat'), may hold values from -3.140625 to 3.140625
- amplitude: float32 [32768], P('feat'), may hold values from 0.4 to 2.3
- doc_weight: float32 [512], P('doc'), may hold values from 0.5 to 4.2
- labels: int32 [512], P('doc'), may hold values from 0 to 127
Outputs:
- margins: float32 [512, 128], P('doc')
- scaled_weights: float32 [32768, 128], P('feat')
All inputs are finite; a program needn't handle non-finite values.
Results may differ from a plain program's by a relative error of at most 0.0003.
Values may be sent and summed in bfloat16 or wider, within the bound.
A program may use at most 64 MiB of HBM per device.

v0:
```python
import jax
import jax.numpy as jnp
from jax import lax
from jax.sharding import PartitionSpec as P

C = 128
ITERS = 3
NEWTON = 3
HI = lax.Precision.HIGHEST
shrink_level = 0.1
ratio_floor = 1e-06


def logistic_prox(target, signs, weight_ratio):
    current = target
    for newton_step in range(NEWTON):
        chance = jax.nn.sigmoid(-signs * current)
        gradient = current - target - weight_ratio * signs * chance
        current = current - gradient / (1.0 + weight_ratio * chance * (1.0 - chance))
    return current


def shrink_values(target, limit):
    return target - jnp.clip(target, -limit, limit)


def per_device(documents, directions, phase, amplitude, doc_weight, labels):
    doc_count = documents.shape[0]
    width_tile = directions.shape[1]
    num_feat = lax.axis_size("feat")
    num_doc = lax.axis_size("doc")
    chunk = width_tile // num_doc
    row = lax.axis_index("doc")
    doc_rows = lax.all_gather(documents, "feat", axis=1, tiled=True)
    doc_full = lax.all_gather(doc_rows, "doc", axis=0, tiled=True)
    dir_chunk = lax.all_to_all(directions, "doc", split_axis=1, concat_axis=0, tiled=True)
    phase_c = lax.dynamic_slice_in_dim(phase, row * chunk, chunk, 0)
    amp_c = lax.dynamic_slice_in_dim(amplitude, row * chunk, chunk, 0)
    angles = jnp.dot(doc_full, dir_chunk, preferred_element_type=jnp.float32)
    features = jnp.sqrt(2.0 / width_tile) * amp_c * jnp.cos(angles + phase_c)
    blocks = features.reshape(num_doc, doc_count, chunk)
    gram = jnp.einsum("iac,ibc->iab", blocks, blocks, precision=HI)
    gram = lax.psum_scatter(gram, "doc", scatter_dimension=0, tiled=True)[0]
    eye = jnp.eye(doc_count, dtype=jnp.float32)
    factor = jnp.linalg.cholesky(eye + gram)
    lower_inv = lax.linalg.triangular_solve(factor, eye, left_side=True, lower=True)
    inverse = lax.dot_general(lower_inv, lower_inv, (((0,), (0,)), ((), ())), precision=HI)
    signs = jnp.where(labels[:, None] == jnp.arange(C, dtype=jnp.int32)[None, :], 1.0, -1.0).astype(
        jnp.float32
    )
    share_rows = doc_count // num_feat
    offset = lax.axis_index("feat") * share_rows
    signs = lax.dynamic_slice_in_dim(signs, offset, share_rows, 0)
    weight = lax.dynamic_slice_in_dim(doc_weight, offset, share_rows, 0)[:, None]
    rho = jnp.float32(1.0)
    margins = logistic_prox(jnp.zeros(signs.shape, jnp.float32), signs, weight / rho)
    sums = jnp.zeros(signs.shape, jnp.float32)
    duals_y = jnp.zeros(signs.shape, jnp.float32)
    part = jnp.zeros((doc_count, C), jnp.float32)
    image = jnp.zeros((doc_count, C), jnp.float32)
    weights = jnp.zeros((chunk, C), jnp.float32)
    product = jnp.zeros((doc_count, C), jnp.float32)
    for step in range(ITERS):
        correction = (margins - duals_y - sums) / num_feat
        correction = lax.all_gather(correction, "feat", axis=0, tiled=True)
        target = part + correction
        residue = target - image
        solved = jnp.dot(inverse, residue, precision=HI)
        applied = residue - solved
        part = target - solved
        sums = lax.psum_scatter(part, "feat", scatter_dimension=0, tiled=True)
        all_solved = lax.all_gather(solved, "doc", axis=0, tiled=True)
        lifted = lax.dot_general(features, all_solved, (((0,), (0,)), ((), ())), precision=HI)
        old_weights = weights
        old_margins = margins
        weights = shrink_values(weights + lifted / num_doc, shrink_level / (rho * num_doc))
        margins = logistic_prox(sums + duals_y, signs, weight / rho)
        duals_y = duals_y + sums - margins
        if step + 1 < ITERS:
            move = old_weights - weights
            if step == 0:
                d_move, d_solved, d_applied, d_lifted = (move, solved, applied, lifted)
            else:
                d_move = move - last_move / growth
                d_solved = solved - last_solved / growth
                d_applied = applied - last_applied / growth
                d_lifted = lifted - last_lifted / growth
            primal = (
                jnp.sum(num_doc * d_move * d_move + 2.0 * d_move * d_lifted)
                + jnp.sum(d_solved * d_applied)
                + jnp.sum((sums - margins) ** 2)
            )
            dual = num_doc * jnp.sum(move**2) + jnp.sum((margins - old_margins) ** 2)
            primal, dual = lax.psum((primal, dual), ("doc", "feat"))
            primal = jnp.maximum(primal, 0.0)
            new_product = jnp.dot(features, weights, precision=HI)
            new_product = lax.psum_scatter(new_product, "doc", scatter_dimension=0, tiled=True)
            growth = ((primal + ratio_floor) / (rho * rho * dual + ratio_floor)) ** 0.25
            rho = rho * growth
            duals_y = duals_y / growth
            image = new_product - (product - new_product + applied) / growth
            product = new_product
            last_move, last_solved, last_applied, last_lifted = (move, solved, applied, lifted)
    margins = lax.all_gather(margins, "feat", axis=0, tiled=True)
    weights = lax.all_gather(num_feat * weights, "doc", axis=0, tiled=True)
    return (margins, weights)


def solution(mesh):
    in_specs = (P("doc", "feat"), P("doc", "feat"), P("feat"), P("feat"), P("doc"), P("doc"))
    out_specs = (P("doc", None), P("feat", None))
    return jax.shard_map(
        per_device, mesh=mesh, in_specs=in_specs, out_specs=out_specs, check_vma=False
    )
```

profile of v0, /device:TPU:0, one launch (start us, length us, event | category | flops | bytes accessed | tf_op | source)
XLA Modules:
  0.0 383.9 jit_solution(2985545460666034803)
XLA Ops:
  7.2 2.3 copy.10
  9.4 6.3 %all-to-all-start = ((bf16[128,4,1024]{0,2,1:T(8,128)(2,1)}), bf16[128,4,1024]{0,2,1:T(8,128)(2,1)S(1)}, u32[]{:S(2)}, u32[]{:S(2)}) async-start(bf16[128,4,1024]{0,2,1:T(8,128)(2,1)} %bitcast), calls=%async_computation | async-start | bytes 2097152 | tf_op jit(solution)/shard_map/all_to_all | solution.py:36
  15.8 9.2 %all_gather.31 = bf16[128,512]{0,1:T(8,128)(2,1)S(1)} all-gather(bf16[128,64]{0,1:T(8,128)(2,1)S(1)} %copy-done.4), channel_id=1, replica_groups=mesh['doc'=4,'feat'=8] {'feat'}, dimensions={1}, use_global_device_ids=true | all-gather | bytes 147456 | tf_op jit(solution)/shard_map/all_gather | solution.py:34
  25.0 0.7 dynamic-slice_multiply_fusion
  25.7 25.3 %all_gather.32 = bf16[512,512]{0,1:T(8,128)(2,1)} all-gather(bf16[128,512]{0,1:T(8,128)(2,1)S(1)} %all_gather.31), channel_id=1, replica_groups=mesh['doc'=4,'feat'=8] {'doc'}, dimensions={0}, use_global_device_ids=true | all-gather | bytes 655360 | tf_op jit(solution)/shard_map/all_gather | solution.py:35
  51.0 0.5 copy.11
  51.6 8.3 %cosine_multiply_fusion = f32[512,1024]{1,0:T(8,128)S(1)} fusion(bf16[512,512]{0,1:T(8,128)(2,1)} %all_gather.32, bf16[512,1024]{1,0:T(8,128)(2,1)S(1)} %bitcast.38, f32[1024]{0:T(1024)S(1)} %dynamic-slice-done, f32[1024]{0:T(1024)S(1)} %dynamic-slice_multiply_fusion), kind=kOutput, calls=%fused_computation | convolution fusion | flops 537919488 | bytes 3678208 | tf_op jit(solution)/shard_map/dot_general | solution.py:39
  59.9 2.8 fusion.142
  62.9 0.1 broadcast_multiply_fusion
  63.1 9.4 %all_gather.30 = f32[128,128]{1,0:T(8,128)S(1)} all-gather(f32[16,128]{1,0:T(8,128)S(1)} %broadcast_multiply_fusion), channel_id=1, replica_groups=mesh['doc'=4,'feat'=8] {'feat'}, dimensions={0}, use_global_device_ids=true | all-gather | bytes 73728 | tf_op jit(solution)/shard_map/all_gather | solution.py:65
  72.5 14.2 %reduce-scatter.7.cloned.1.call-done = f32[1,128,128]{2,1,0:T(8,128)} async-done(((f32[4,128,128]{2,1,0:T(8,128)}), f32[1,128,128]{2,1,0:T(8,128)}) %reduce-scatter.7.cloned.1.call-update) | async-done | bytes 65552 | tf_op jit(solution)/shard_map/reduce_scatter | solution.py:43
  86.7 0.9 bitcast_add_fusion.1
  87.6 0.9 fusion.13
  88.5 11.7 %cholesky.18 = f32[128,128]{1,0:T(8,128)S(1)} custom-call(f32[128,128]{1,0:T(8,128)S(1)} %fusion.13), custom_call_target="Cholesky" | custom-call | tf_op jit(solution)/shard_map/jit(cholesky)/cholesky | solution.py:45
  100.2 0.6 compare_reduce_fusion
  100.9 0.7 fusion.10
  101.6 9.8 %custom-call.6 = f32[1,128,128]{1,2,0:T(8,128)S(1)} custom-call(f32[1,128,128]{2,1,0:T(8,128)S(1)} %fusion.10), custom_call_target="InvertDiagBlocksLowerTriangular" | custom-call | tf_op jit(solution)/shard_map/triangular_solve | solution.py:46
  111.4 0.3 fusion.11
  111.6 0.3 fusion.143
  111.9 1.5 multiply_reduce_fusion.3
  113.5 14.1 %all_gather.33 = f32[512,128]{1,0:T(8,128)S(1)} all-gather(f32[128,128]{1,0:T(8,128)S(1)} %get-tuple-element.23), channel_id=1, replica_groups=mesh['doc'=4,'feat'=8] {'doc'}, dimensions={0}, use_global_device_ids=true | all-gather | bytes 327680 | tf_op jit(solution)/shard_map/all_gather | solution.py:72
  127.6 4.1 %multiply_reduce_fusion.1 = (f32[]{:T(128)}, f32[]{:T(128)}, f32[1024,128]{1,0:T(8,128)S(1)}) fusion(f32[512,1024]{1,0:T(8,128)S(1)} %cosine_multiply_fusion, f32[512,128]{1,0:T(8,128)S(1)} %all_gather.33), kind=kOutput, calls=%fused_computation.13 | convolution fusion | flops 806879232 | bytes 2883592 | tf_op jit(solution)/shard_map/dot_general | solution.py:73
  131.7 2.5 fusion.6
  136.2 9.2 %reduce-scatter.9.cloned.1.call-done = f32[16,128]{1,0:T(8,128)} async-done(((f32[128,128]{1,0:T(8,128)}), f32[16,128]{1,0:T(8,128)}) %reduce-scatter.9.cloned.1.call-update) | async-done | bytes 8208 | tf_op jit(solution)/shard_map/reduce_scatter | solution.py:71
  145.4 1.5 multiply_reduce_fusion.6
  146.8 1.3 multiply_reduce_fusion.7
  149.3 39.3 %all-reduce.1 = (f32[]{:T(128)}, f32[]{:T(128)}) all-reduce(f32[]{:T(128)S(6)} %add.203, f32[]{:T(128)S(6)} %add.205), channel_id=1, replica_groups=mesh['doc'=4,'feat'=8] {'doc','feat'}, use_global_device_ids=true, to_apply=%region_7.8 | all-reduce | flops 2 | bytes 16 | tf_op jit(solution)/shard_map/psum | solution.py:94
  189.9 0.7 subtract_multiply_fusion.2
  190.6 10.2 %all_gather.34 = f32[128,128]{1,0:T(8,128)S(1)} all-gather(f32[16,128]{1,0:T(8,128)S(1)} %subtract_multiply_fusion.2), channel_id=1, replica_groups=mesh['doc'=4,'feat'=8] {'feat'}, dimensions={0}, use_global_device_ids=true | all-gather | bytes 73728 | tf_op jit(solution)/shard_map/all_gather | solution.py:65
  200.8 0.9 subtract_subtract_fusion
  201.7 1.5 multiply_reduce_fusion.2
  203.2 14.2 %all_gather.35 = f32[512,128]{1,0:T(8,128)S(1)} all-gather(f32[128,128]{1,0:T(8,128)S(1)} %get-tuple-element.25), channel_id=1, replica_groups=mesh['doc'=4,'feat'=8] {'doc'}, dimensions={0}, use_global_device_ids=true | all-gather | bytes 327680 | tf_op jit(solution)/shard_map/all_gather | solution.py:72
  217.4 4.2 %multiply_reduce_fusion = (f32[]{:T(128)}, f32[]{:T(128)}, f32[1024,128]{1,0:T(8,128)S(1)}) fusion(f32[1024,128]{1,0:T(8,128)S(1)} %get-tuple-element.24, f32[]{:T(128)S(6)} %neg.66, f32[]{:T(128)S(6)} %div.199, f32[]{:T(128)S(6)} %pow.6, f32[512,1024]{1,0:T(8,128)S(1)} %cosine_multiply_fusion, f32[512,128]{1,0:T(8,128)S(1)} %all_gather.35), kind=kOutput, calls=%fused_computation.11 | convolution fusion | flops 808189952 | bytes 3407892 | tf_op jit(solution)/shard_map/dot_general | solution.py:73
  221.6 2.5 fusion.137
  226.1 9.7 %reduce-scatter.13.cloned.1.call-done = f32[16,128]{1,0:T(8,128)} async-done(((f32[128,128]{1,0:T(8,128)}), f32[16,128]{1,0:T(8,128)}) %reduce-scatter.13.cloned.1.call-update) | async-done | bytes 8208 | tf_op jit(solution)/shard_map/reduce_scatter | solution.py:71
  235.9 1.5 multiply_reduce_fusion.4
  238.5 39.4 %all-reduce = (f32[]{:T(128)}, f32[]{:T(128)}) all-reduce(f32[]{:T(128)S(6)} %add.219, f32[]{:T(128)S(6)} %add.221), channel_id=1, replica_groups=mesh['doc'=4,'feat'=8] {'doc','feat'}, use_global_device_ids=true, to_apply=%region_16.17 | all-reduce | flops 2 | bytes 16 | tf_op jit(solution)/shard_map/psum | solution.py:94
  279.2 0.7 subtract_multiply_fusion.1
  279.9 11.2 %all_gather.36 = f32[128,128]{1,0:T(8,128)} all-gather(f32[16,128]{1,0:T(8,128)S(1)} %subtract_multiply_fusion.1), channel_id=1, replica_groups=mesh['doc'=4,'feat'=8] {'feat'}, dimensions={0}, use_global_device_ids=true | all-gather | bytes 73728 | tf_op jit(solution)/shard_map/all_gather | solution.py:65
  291.1 1.8 fusion.140
  292.9 14.0 %all_gather.38 = f32[512,128]{1,0:T(8,128)S(1)} all-gather(f32[128,128]{1,0:T(8,128)S(1)} %get-tuple-element.28), channel_id=1, replica_groups=mesh['doc'=4,'feat'=8] {'doc'}, dimensions={0}, use_global_device_ids=true | all-gather | bytes 327680 | tf_op jit(solution)/shard_map/all_gather | solution.py:72
  306.9 4.2 %subtract_multiply_fusion = f32[1024,128]{1,0:T(8,128)} fusion(f32[512,1024]{1,0:T(8,128)S(1)} %cosine_multiply_fusion, f32[512,128]{1,0:T(8,128)S(1)} %all_gather.38, f32[]{:T(128)S(6)} %neg.70, f32[]{:T(128)S(6)} %div.220, f32[]{:T(128)S(6)} %neg.66, f32[]{:T(128)S(6)} %div.199, f32[1024,128]{1,0:T(8,128)S(1)} %get-tuple-element.26, ...), kind=kOutput, calls=%fused_computation.10 | convolution fusion | flops 807141376 | bytes 3932176 | tf_op jit(solution)/shard_map/dot_general | solution.py:73
  311.2 14.3 %reduce-scatter.17.cloned.1.call-done = f32[16,128]{1,0:T(8,128)} async-done(((f32[128,128]{1,0:T(8,128)}), f32[16,128]{1,0:T(8,128)}) %reduce-scatter.17.cloned.1.call-update) | async-done | bytes 8208 | tf_op jit(solution)/shard_map/reduce_scatter | solution.py:71
  325.6 0.8 fusion.63
  326.4 9.2 %all_gather.37 = f32[128,128]{1,0:T(8,128)S(1)} all-gather(f32[16,128]{1,0:T(8,128)S(1)} %fusion.63), channel_id=1, replica_groups=mesh['doc'=4,'feat'=8] {'feat'}, dimensions={0}, use_global_device_ids=true | all-gather | bytes 73728 | tf_op jit(solution)/shard_map/all_gather | solution.py:104
  335.6 37.8 %all-gather.2.cloned.1.call-done = f32[4096,128]{1,0:T(8,128)} async-done(((f32[1024,128]{1,0:T(8,128)}), f32[4096,128]{1,0:T(8,128)}) %all-gather.2.cloned.1.call-update) | async-done | bytes 2097168 | tf_op jit(solution)/shard_map/all_gather | solution.py:105
  373.4 0.6 copy.15
  374.0 3.0 copy.16
  (45 shorter events, 0.9 us)
Async XLA Ops:
  7.2 8.6 %copy-start.4 = (bf16[128,64]{0,1:T(8,128)(2,1)S(1)}, bf16[128,64]{0,1:T(8,128)(2,1)}, u32[]{:S(2)}) copy-start(bf16[128,64]{0,1:T(8,128)(2,1)} %param.6) | copy-start | bytes 49156
  9.4 41.6 %all-to-all-start = ((bf16[128,4,1024]{0,2,1:T(8,128)(2,1)}), bf16[128,4,1024]{0,2,1:T(8,128)(2,1)S(1)}, u32[]{:S(2)}, u32[]{:S(2)}) async-start(bf16[128,4,1024]{0,2,1:T(8,128)(2,1)} %bitcast), calls=%async_computation | async-start | bytes 2097152 | tf_op jit(solution)/shard_map/all_to_all | solution.py:36
  15.8 70.9 %reduce-scatter.7.cloned.1.call-start = ((), (), s32[]{:S(2)}) async-start(), calls=%async_computation.7 | async-start | bytes 327680 | tf_op jit(solution)/shard_map/reduce_scatter | solution.py:43
  15.8 35.8 %dynamic-slice-start = ((f32[4096]{0:T(1024)}, s32[]{:T(128)}), f32[1024]{0:T(1024)S(1)}, s32[]{:S(2)}) async-start(f32[4096]{0:T(1024)} %param.8, s32[]{:T(128)} %select_n.18), calls=%async_computation.14 | async-start | bytes 8704 | tf_op jit(solution)/shard_map/dynamic_slice | solution.py:37
  59.9 2.9 copy-start.9
  59.9 2.9 copy-start.7
  62.7 82.6 %reduce-scatter.9.cloned.1.call-start = ((), (), s32[]{:S(2)}) async-start(), calls=%async_computation.8 | async-start | bytes 73728 | tf_op jit(solution)/shard_map/reduce_scatter | solution.py:71
  62.9 173.0 %copy-start.5 = (s32[16]{0:T(128)}, s32[16]{0:T(128)S(1)}, u32[]{:S(2)}) copy-start(s32[16]{0:T(128)S(1)} %dynamic-slice) | copy-start | bytes 196
  113.5 87.4 %reduce-scatter.11.cloned.1.call-start = ((), (), s32[]{:S(2)}) async-start(), calls=%async_computation.9 | async-start | bytes 327680 | tf_op jit(solution)/shard_map/reduce_scatter | solution.py:97
  131.7 69.2 %copy-start = (f32[128,128]{1,0:T(8,128)S(1)}, f32[128,128]{1,0:T(8,128)}, u32[]{:S(2)}) copy-start(f32[128,128]{1,0:T(8,128)} %get-tuple-element.20) | copy-start | bytes 196612
  136.1 99.8 %reduce-scatter.13.cloned.1.call-start = ((), (), s32[]{:S(2)}) async-start(), calls=%async_computation.10 | async-start | bytes 73728 | tf_op jit(solution)/shard_map/reduce_scatter | solution.py:71
  203.2 87.9 %reduce-scatter.15.cloned.1.call-start = ((), (), s32[]{:S(2)}) async-start(), calls=%async_computation.11 | async-start | bytes 327680 | tf_op jit(solution)/shard_map/reduce_scatter | solution.py:97
  221.6 69.5 %copy-start.1 = (f32[128,128]{1,0:T(8,128)S(1)}, f32[128,128]{1,0:T(8,128)}, u32[]{:S(2)}) copy-start(f32[128,128]{1,0:T(8,128)} %reduce-scatter.11.cloned.1.call-done) | copy-start | bytes 196612
  221.6 69.5 %copy-start.2 = (f32[128,128]{1,0:T(8,128)S(1)}, f32[128,128]{1,0:T(8,128)}, u32[]{:S(2)}) copy-start(f32[128,128]{1,0:T(8,128)} %get-tuple-element.22) | copy-start | bytes 196612
  224.2 101.4 %reduce-scatter.17.cloned.1.call-start = ((), (), s32[]{:S(2)}) async-start(), calls=%async_computation.12 | async-start | bytes 73728 | tf_op jit(solution)/shard_map/reduce_scatter | solution.py:71
  292.9 80.5 %all-gather.2.cloned.1.call-start = ((), (), s32[]{:S(2)}) async-start(), calls=%async_computation.13 | async-start | bytes 2621440 | tf_op jit(solution)/shard_map/all_gather | solution.py:105
  306.9 4.3 %copy-start.8 = (f32[128]{0:T(128)S(1)}, f32[128]{0:T(128)}, u32[]{:S(2)}) copy-start(f32[128]{0:T(128)} %param.10) | copy-start | bytes 1540
  306.9 18.7 %copy-start.3 = (f32[16,128]{1,0:T(8,128)S(1)}, f32[16,128]{1,0:T(8,128)}, u32[]{:S(2)}) copy-start(f32[16,128]{1,0:T(8,128)} %reduce-scatter.13.cloned.1.call-done) | copy-start | bytes 24580
  306.9 18.7 %copy-start.6 = (s32[16]{0:T(128)S(1)}, s32[16]{0:T(128)}, u32[]{:S(2)}) copy-start(s32[16]{0:T(128)} %copy-done.5) | copy-start | bytes 196
Sparse Core Ops, SparseCore 0:
  62.8 23.8 reduce-scatter.6
  113.6 31.7 reduce-scatter.8
  148.2 19.9 reduce-scatter.10
  203.3 32.4 reduce-scatter.12
  238.5 19.9 reduce-scatter.14
  293.0 32.5 reduce-scatter.16
  327.7 45.6 all-gather.1
where the time goes:
time: 385 us; the launch traced here: 384 us
  blocking collectives  195 us (51%)
  waiting for transfers between devices  85.3 us (22%)
  matrix products  33.9 us (9%)
  other arithmetic  32.9 us (9%)
  between operations  23 us (6%)
  local copies, waits for them, and re-layouts  6.75 us (2%)
  starting transfers between devices  6.6 us (2%)
    psum x2, blocking collectives, per_device(): primal, dual = lax.psum((primal, dual), ('doc', 'feat'))  78.7 us
    all_gather x3, blocking collectives, per_device(): all_solved = lax.all_gather(solved, 'doc', axis=0, tiled=True)  42.2 us
    all_gather x1, waiting for transfers between devices, per_device(): weights = lax.all_gather(num_feat * weights, 'doc', axis=0, tiled=True)  37.8 us
    reduce_scatter x3, waiting for transfers between devices, per_device(): sums = lax.psum_scatter(part, 'feat', scatter_dimension=0, tiled=True)  33.2 us
    all_gather x3, blocking collectives, per_device(): correction = lax.all_gather(correction, 'feat', axis=0, tiled=True)  30.8 us
    all_gather x1, blocking collectives, per_device(): doc_full = lax.all_gather(doc_rows, 'doc', axis=0, tiled=True)  25.3 us
    reduce_scatter x1, waiting for transfers between devices, per_device(): gram = lax.psum_scatter(gram, 'doc', scatter_dimension=0, tiled=True)[0]  14.2 us
    dot_general x3, matrix products, per_device(): lax.dot_general(features, all_solved, (((0,), (0,)), ((), ())), precision...  12.5 us
  transfers between devices with their start and end apart: 8, of which 5 were waited for; matrix products, arithmetic and copies ran while one was open for 7% of the time, Pallas kernels for 0%

commit v1 on v0

--- a/solution.py
+++ b/solution.py
@@ -69,7 +69,14 @@
         applied = residue - solved
         part = target - solved
         sums = lax.psum_scatter(part, "feat", scatter_dimension=0, tiled=True)
-        all_solved = lax.all_gather(solved, "doc", axis=0, tiled=True)
+        ring = [solved]
+        for hop in range(3):
+            ring.append(lax.ppermute(ring[-1], "doc", [(dev, (dev + 1) % 4) for dev in range(4)]))
+        all_solved = jnp.roll(
+            jnp.concatenate(ring[::-1], axis=0),
+            (lax.axis_index("doc") + 1) * ring[0].shape[0],
+            axis=0,
+        )
         lifted = lax.dot_general(features, all_solved, (((0,), (0,)), ((), ())), precision=HI)
         old_weights = weights
         old_margins = margins

time: 385 us -> 431 us (1.12)
  waiting for transfers between devices: 85.3 us -> 169 us
  blocking collectives: 195 us -> 152 us
    ppermute x0 -> x9, waiting for transfers between devices: none -> 51.6 us  [per_device(): lax.ppermute(ring[-1], 'doc', [(dev, (dev + 1) % 4) for dev in range(4)])]
    all_gather x3 -> x0, blocking collectives: 42.2 us -> none  [per_device(): all_solved = lax.all_gather(solved, 'doc', axis=0, tiled=True)]
    reduce_scatter x3, waiting for transfers between devices: 33.2 us -> 65.4 us  [per_device(): sums = lax.psum_scatter(part, 'feat', scatter_dimension=0, tiled=True)]
  transfers between devices with their start and end apart: 8 -> 17, of which waited for: 5 -> 14; matrix products, arithmetic and copies ran while one was open for 7% -> 6% of each run, Pallas kernels for 0% -> 0%
where the time goes in v1:
time: 431 us; the launch traced here: 430 us
  waiting for transfers between devices  169 us (39%)
  blocking collectives  152 us (35%)
  matrix products  35.7 us (8%)
  other arithmetic  33 us (8%)
  between operations  23.2 us (5%)
  starting transfers between devices  10 us (2%)
  local copies, waits for them, and re-layouts  6.76 us (2%)
    psum x2, blocking collectives, per_device(): primal, dual = lax.psum((primal, dual), ('doc', 'feat'))  78.6 us
    reduce_scatter x3, waiting for transfers between devices, per_device(): sums = lax.psum_scatter(part, 'feat', scatter_dimension=0, tiled=True)  65.4 us
    ppermute x9, waiting for transfers between devices, per_device(): lax.ppermute(ring[-1], 'doc', [(dev, (dev + 1) % 4) for dev in range(4)])  51.6 us
    all_gather x1, waiting for transfers between devices, per_device(): weights = lax.all_gather(num_feat * weights, 'doc', axis=0, tiled=True)  37.8 us
    all_gather x3, blocking collectives, per_device(): correction = lax.all_gather(correction, 'feat', axis=0, tiled=True)  29.9 us
    all_gather x1, blocking collectives, per_device(): doc_full = lax.all_gather(doc_rows, 'doc', axis=0, tiled=True)  25.3 us
    dot_general x3, matrix products, per_device(): lax.dot_general(features, all_solved, (((0,), (0,)), ((), ())), precision...  14.4 us
    reduce_scatter x1, waiting for transfers between devices, per_device(): gram = lax.psum_scatter(gram, 'doc', scatter_dimension=0, tiled=True)[0]  14.2 us
  transfers between devices with their start and end apart: 17, of which 14 were waited for; matrix products, arithmetic and copies ran while one was open for 6% of the time, Pallas kernels for 0%

profile of v1, /device:TPU:0, one launch (start us, length us, event | category | flops | bytes accessed | tf_op | source)
XLA Modules:
  0.0 430.0 jit_solution(1048997528707711899)
XLA Ops:
  7.2 2.3 copy.10
  9.4 6.3 %all-to-all-start = ((bf16[128,4,1024]{0,2,1:T(8,128)(2,1)}), bf16[128,4,1024]{0,2,1:T(8,128)(2,1)S(1)}, u32[]{:S(2)}, u32[]{:S(2)}) async-start(bf16[128,4,1024]{0,2,1:T(8,128)(2,1)} %bitcast), calls=%async_computation | async-start | bytes 2097152 | tf_op jit(solution)/shard_map/all_to_all | solution.py:36
  15.8 9.2 %all_gather.22 = bf16[128,512]{0,1:T(8,128)(2,1)S(1)} all-gather(bf16[128,64]{0,1:T(8,128)(2,1)S(1)} %copy-done.7), channel_id=1, replica_groups=mesh['doc'=4,'feat'=8] {'feat'}, dimensions={1}, use_global_device_ids=true | all-gather | bytes 147456 | tf_op jit(solution)/shard_map/all_gather | solution.py:34
  25.7 25.3 %all_gather.23 = bf16[512,512]{0,1:T(8,128)(2,1)} all-gather(bf16[128,512]{0,1:T(8,128)(2,1)S(1)} %all_gather.22), channel_id=1, replica_groups=mesh['doc'=4,'feat'=8] {'doc'}, dimensions={0}, use_global_device_ids=true | all-gather | bytes 655360 | tf_op jit(solution)/shard_map/all_gather | solution.py:35
  51.6 8.3 %cosine_multiply_fusion = f32[512,1024]{1,0:T(8,128)S(1)} fusion(bf16[512,512]{0,1:T(8,128)(2,1)} %all_gather.23, bf16[512,1024]{1,0:T(8,128)(2,1)S(1)} %bitcast.35, f32[1024]{0:T(1024)S(1)} %dynamic-slice-done, f32[1024]{0:T(1024)S(1)} %dynamic-slice_multiply_fusion), kind=kOutput, calls=%fused_computation | convolution fusion | flops 537919488 | bytes 3678208 | tf_op jit(solution)/shard_map/dot_general | solution.py:39
  59.9 2.8 fusion.177
  63.1 9.4 %all_gather.21 = f32[128,128]{1,0:T(8,128)S(1)} all-gather(f32[16,128]{1,0:T(8,128)S(1)} %broadcast_multiply_fusion), channel_id=1, replica_groups=mesh['doc'=4,'feat'=8] {'feat'}, dimensions={0}, use_global_device_ids=true | all-gather | bytes 73728 | tf_op jit(solution)/shard_map/all_gather | solution.py:65
  72.5 14.2 %reduce-scatter.7.cloned.1.call-done = f32[1,128,128]{2,1,0:T(8,128)} async-done(((f32[4,128,128]{2,1,0:T(8,128)}), f32[1,128,128]{2,1,0:T(8,128)}) %reduce-scatter.7.cloned.1.call-update) | async-done | bytes 65552 | tf_op jit(solution)/shard_map/reduce_scatter | solution.py:43
  86.7 0.9 bitcast_add_fusion.1
  87.6 0.9 fusion.42
  88.5 11.7 %cholesky.18 = f32[128,128]{1,0:T(8,128)S(1)} custom-call(f32[128,128]{1,0:T(8,128)S(1)} %fusion.42), custom_call_target="Cholesky" | custom-call | tf_op jit(solution)/shard_map/jit(cholesky)/cholesky | solution.py:45
  101.6 9.8 %custom-call.6 = f32[1,128,128]{1,2,0:T(8,128)S(1)} custom-call(f32[1,128,128]{2,1,0:T(8,128)S(1)} %fusion.39), custom_call_target="InvertDiagBlocksLowerTriangular" | custom-call | tf_op jit(solution)/shard_map/triangular_solve | solution.py:46
  111.9 1.4 multiply_reduce_fusion.3
  113.4 6.1 %collective-permute-done = f32[128,128]{1,0:T(8,128)S(1)} collective-permute-done((f32[128,128]{1,0:T(8,128)S(1)}, f32[128,128]{1,0:T(8,128)S(1)}, u32[]{:S(2)}, u32[]{:S(2)}) %collective-permute-start) | collective-permute-done | bytes 65568 | tf_op jit(solution)/shard_map/ppermute | solution.py:74
  119.4 6.5 %collective-permute-done.1 = f32[128,128]{1,0:T(8,128)S(1)} collective-permute-done((f32[128,128]{1,0:T(8,128)S(1)}, f32[128,128]{1,0:T(8,128)S(1)}, u32[]{:S(2)}, u32[]{:S(2)}) %collective-permute-start.1) | collective-permute-done | bytes 65568 | tf_op jit(solution)/shard_map/ppermute | solution.py:74
  126.3 5.8 %collective-permute-done.2 = f32[128,128]{1,0:T(8,128)S(1)} collective-permute-done((f32[128,128]{1,0:T(8,128)S(1)}, f32[128,128]{1,0:T(8,128)S(1)}, u32[]{:S(2)}, u32[]{:S(2)}) %collective-permute-start.2) | collective-permute-done | bytes 65568 | tf_op jit(solution)/shard_map/ppermute | solution.py:74
  132.0 4.5 %multiply_reduce_fusion.1 = (f32[]{:T(128)}, f32[]{:T(128)}, f32[1024,128]{1,0:T(8,128)S(1)}) fusion(f32[512,1024]{1,0:T(8,128)S(1)} %cosine_multiply_fusion, s32[]{:T(128)S(6)} %select_n.35, f32[128,128]{1,0:T(8,128)S(1)} %collective-permute-done.2, f32[128,128]{1,0:T(8,128)S(1)} %collective-permute-done.1, f32[128,128]{1,0:T(8,128)S(1)} %collective-permute-done, ...), kind=kOutput, calls=%fused_computation.37 | convolution fusion | flops 807337984 | bytes 2883596 | tf_op jit(solution)/shard_map/dot_general | solution.py:80
  136.5 2.5 fusion.6
  139.1 21.9 %reduce-scatter.9.cloned.1.call-done = f32[16,128]{1,0:T(8,128)} async-done(((f32[128,128]{1,0:T(8,128)}), f32[16,128]{1,0:T(8,128)}) %reduce-scatter.9.cloned.1.call-update) | async-done | bytes 8208 | tf_op jit(solution)/shard_map/reduce_scatter | solution.py:71
  161.0 1.4 multiply_reduce_fusion.6
  162.5 1.4 multiply_reduce_fusion.7
  167.0 39.3 %all-reduce.1 = (f32[]{:T(128)}, f32[]{:T(128)}) all-reduce(f32[]{:T(128)S(6)} %add.217, f32[]{:T(128)S(6)} %add.219), channel_id=1, replica_groups=mesh['doc'=4,'feat'=8] {'doc','feat'}, use_global_device_ids=true, to_apply=%region_7.9 | all-reduce | flops 2 | bytes 16 | tf_op jit(solution)/shard_map/psum | solution.py:101
  207.6 0.7 subtract_multiply_fusion.2
  208.3 10.2 %all_gather.24 = f32[128,128]{1,0:T(8,128)S(1)} all-gather(f32[16,128]{1,0:T(8,128)S(1)} %subtract_multiply_fusion.2), channel_id=1, replica_groups=mesh['doc'=4,'feat'=8] {'feat'}, dimensions={0}, use_global_device_ids=true | all-gather | bytes 73728 | tf_op jit(solution)/shard_map/all_gather | solution.py:65
  218.5 0.9 subtract_subtract_fusion
  219.3 1.4 multiply_reduce_fusion.2
  220.8 1.5 collective-permute-start.3
  222.2 4.7 %collective-permute-done.3 = f32[128,128]{1,0:T(8,128)S(1)} collective-permute-done((f32[128,128]{1,0:T(8,128)S(1)}, f32[128,128]{1,0:T(8,128)S(1)}, u32[]{:S(2)}, u32[]{:S(2)}) %collective-permute-start.3) | collective-permute-done | bytes 65568 | tf_op jit(solution)/shard_map/ppermute | solution.py:74
  226.9 6.1 %collective-permute-done.4 = f32[128,128]{1,0:T(8,128)S(1)} collective-permute-done((f32[128,128]{1,0:T(8,128)S(1)}, f32[128,128]{1,0:T(8,128)S(1)}, u32[]{:S(2)}, u32[]{:S(2)}) %collective-permute-start.4) | collective-permute-done | bytes 65568 | tf_op jit(solution)/shard_map/ppermute | solution.py:74
  233.4 5.8 %collective-permute-done.5 = f32[128,128]{1,0:T(8,128)} collective-permute-done((f32[128,128]{1,0:T(8,128)S(1)}, f32[128,128]{1,0:T(8,128)}, u32[]{:S(2)}, u32[]{:S(2)}) %collective-permute-start.5) | collective-permute-done | bytes 65568 | tf_op jit(solution)/shard_map/ppermute | solution.py:74
  239.2 5.3 %multiply_reduce_fusion = (f32[]{:T(128)}, f32[]{:T(128)}, f32[1024,128]{1,0:T(8,128)S(1)}) fusion(f32[1024,128]{1,0:T(8,128)S(1)} %get-tuple-element.25, f32[]{:T(128)S(6)} %neg.66, f32[]{:T(128)S(6)} %div.199, f32[]{:T(128)S(6)} %pow.6, f32[512,1024]{1,0:T(8,128)S(1)} %cosine_multiply_fusion, s32[]{:T(128)S(6)} %select_n.35, ...), kind=kOutput, calls=%fused_computation.35 | convolution fusion | flops 808648704 | bytes 3407896 | tf_op jit(solution)/shard_map/dot_general | solution.py:80
  244.5 2.5 fusion.172
  247.2 20.0 %reduce-scatter.13.cloned.1.call-done = f32[16,128]{1,0:T(8,128)} async-done(((f32[128,128]{1,0:T(8,128)}), f32[16,128]{1,0:T(8,128)}) %reduce-scatter.13.cloned.1.call-update) | async-done | bytes 8208 | tf_op jit(solution)/shard_map/reduce_scatter | solution.py:71
  267.3 1.5 multiply_reduce_fusion.4
  271.8 39.3 %all-reduce = (f32[]{:T(128)}, f32[]{:T(128)}) all-reduce(f32[]{:T(128)S(6)} %add.233, f32[]{:T(128)S(6)} %add.235), channel_id=1, replica_groups=mesh['doc'=4,'feat'=8] {'doc','feat'}, use_global_device_ids=true, to_apply=%region_16.18 | all-reduce | flops 2 | bytes 16 | tf_op jit(solution)/shard_map/psum | solution.py:101
  312.4 0.7 subtract_multiply_fusion.1
  313.2 10.2 %all_gather.25 = f32[128,128]{1,0:T(8,128)S(1)} all-gather(f32[16,128]{1,0:T(8,128)S(1)} %subtract_multiply_fusion.1), channel_id=1, replica_groups=mesh['doc'=4,'feat'=8] {'feat'}, dimensions={0}, use_global_device_ids=true | all-gather | bytes 73728 | tf_op jit(solution)/shard_map/all_gather | solution.py:65
  323.4 1.7 fusion.175
  325.1 1.5 collective-permute-start.6
  326.6 4.7 %collective-permute-done.6 = f32[128,128]{1,0:T(8,128)S(1)} collective-permute-done((f32[128,128]{1,0:T(8,128)S(1)}, f32[128,128]{1,0:T(8,128)S(1)}, u32[]{:S(2)}, u32[]{:S(2)}) %collective-permute-start.6) | collective-permute-done | bytes 65568 | tf_op jit(solution)/shard_map/ppermute | solution.py:74
  331.3 6.1 %collective-permute-done.7 = f32[128,128]{1,0:T(8,128)S(1)} collective-permute-done((f32[128,128]{1,0:T(8,128)S(1)}, f32[128,128]{1,0:T(8,128)S(1)}, u32[]{:S(2)}, u32[]{:S(2)}) %collective-permute-start.7) | collective-permute-done | bytes 65568 | tf_op jit(solution)/shard_map/ppermute | solution.py:74
  337.6 5.9 %collective-permute-done.8 = f32[128,128]{1,0:T(8,128)S(1)} collective-permute-done((f32[128,128]{1,0:T(8,128)S(1)}, f32[128,128]{1,0:T(8,128)S(1)}, u32[]{:S(2)}, u32[]{:S(2)}) %collective-permute-start.8) | collective-permute-done | bytes 65568 | tf_op jit(solution)/shard_map/ppermute | solution.py:74
  343.5 4.6 %subtract_multiply_fusion = f32[1024,128]{1,0:T(8,128)} fusion(f32[512,1024]{1,0:T(8,128)S(1)} %cosine_multiply_fusion, s32[]{:T(128)S(6)} %select_n.35, f32[128,128]{1,0:T(8,128)S(1)} %collective-permute-done.8, f32[128,128]{1,0:T(8,128)S(1)} %collective-permute-done.7, f32[128,128]{1,0:T(8,128)S(1)} %collective-permute-done.6, ...), kind=kOutput, calls=%fused_computation.34 | convolution fusion | flops 807600128 | bytes 3932180 | tf_op jit(solution)/shard_map/dot_general | solution.py:80
  348.2 23.5 %reduce-scatter.17.cloned.1.call-done = f32[16,128]{1,0:T(8,128)} async-done(((f32[128,128]{1,0:T(8,128)}), f32[16,128]{1,0:T(8,128)}) %reduce-scatter.17.cloned.1.call-update) | async-done | bytes 8208 | tf_op jit(solution)/shard_map/reduce_scatter | solution.py:71
  371.6 0.8 fusion.92
  372.5 9.2 %all_gather.26 = f32[128,128]{1,0:T(8,128)S(1)} all-gather(f32[16,128]{1,0:T(8,128)S(1)} %fusion.92), channel_id=1, replica_groups=mesh['doc'=4,'feat'=8] {'feat'}, dimensions={0}, use_global_device_ids=true | all-gather | bytes 73728 | tf_op jit(solution)/shard_map/all_gather | solution.py:111
  381.7 37.8 %all-gather.2.cloned.1.call-done = f32[4096,128]{1,0:T(8,128)} async-done(((f32[1024,128]{1,0:T(8,128)}), f32[4096,128]{1,0:T(8,128)}) %all-gather.2.cloned.1.call-update) | async-done | bytes 2097168 | tf_op jit(solution)/shard_map/all_gather | solution.py:112
  420.1 3.0 copy.16
  (66 shorter events, 5.2 us)
Async XLA Ops:
  7.2 8.6 %copy-start.7 = (bf16[128,64]{0,1:T(8,128)(2,1)S(1)}, bf16[128,64]{0,1:T(8,128)(2,1)}, u32[]{:S(2)}) copy-start(bf16[128,64]{0,1:T(8,128)(2,1)} %param.8) | copy-start | bytes 49156
  9.4 41.6 %all-to-all-start = ((bf16[128,4,1024]{0,2,1:T(8,128)(2,1)}), bf16[128,4,1024]{0,2,1:T(8,128)(2,1)S(1)}, u32[]{:S(2)}, u32[]{:S(2)}) async-start(bf16[128,4,1024]{0,2,1:T(8,128)(2,1)} %bitcast), calls=%async_computation | async-start | bytes 2097152 | tf_op jit(solution)/shard_map/all_to_all | solution.py:36
  15.8 70.9 %reduce-scatter.7.cloned.1.call-start = ((), (), s32[]{:S(2)}) async-start(), calls=%async_computation.7 | async-start | bytes 327680 | tf_op jit(solution)/shard_map/reduce_scatter | solution.py:43
  15.8 35.8 %dynamic-slice-start = ((f32[4096]{0:T(1024)}, s32[]{:T(128)}), f32[1024]{0:T(1024)S(1)}, s32[]{:S(2)}) async-start(f32[4096]{0:T(1024)} %param.10, s32[]{:T(128)} %select_n.28), calls=%async_computation.14 | async-start | bytes 8704 | tf_op jit(solution)/shard_map/dynamic_slice | solution.py:37
  59.9 2.9 copy-start.12
  59.9 2.9 copy-start.10
  62.7 98.3 %reduce-scatter.9.cloned.1.call-start = ((), (), s32[]{:S(2)}) async-start(), calls=%async_computation.8 | async-start | bytes 73728 | tf_op jit(solution)/shard_map/reduce_scatter | solution.py:71
  62.9 204.4 %copy-start.8 = (s32[16]{0:T(128)}, s32[16]{0:T(128)S(1)}, u32[]{:S(2)}) copy-start(s32[16]{0:T(128)S(1)} %dynamic-slice) | copy-start | bytes 196
  113.4 6.1 %collective-permute-start = (f32[128,128]{1,0:T(8,128)S(1)}, f32[128,128]{1,0:T(8,128)S(1)}, u32[]{:S(2)}, u32[]{:S(2)}) collective-permute-start(f32[128,128]{1,0:T(8,128)S(1)} %get-tuple-element.24), channel_id=1, source_target_pairs={{0,8},{8,16},{16,24},{24,0},{1,9},{9,17},{17,25},{25,1},{2,10},{10... | collective-permute-start | bytes 196616 | tf_op jit(solution)/shard_map/ppermute | solution.py:74
  119.4 6.6 %collective-permute-start.1 = (f32[128,128]{1,0:T(8,128)S(1)}, f32[128,128]{1,0:T(8,128)S(1)}, u32[]{:S(2)}, u32[]{:S(2)}) collective-permute-start(f32[128,128]{1,0:T(8,128)S(1)} %collective-permute-done), channel_id=1, source_target_pairs={{0,8},{8,16},{16,24},{24,0},{1,9},{9,17},{17,25},{25,1},{2,10},{10... | collective-permute-start | bytes 196616 | tf_op jit(solution)/shard_map/ppermute | solution.py:74
  126.0 6.1 %collective-permute-start.2 = (f32[128,128]{1,0:T(8,128)S(1)}, f32[128,128]{1,0:T(8,128)S(1)}, u32[]{:S(2)}, u32[]{:S(2)}) collective-permute-start(f32[128,128]{1,0:T(8,128)S(1)} %collective-permute-done.1), channel_id=1, source_target_pairs={{0,8},{8,16},{16,24},{24,0},{1,9},{9,17},{17,25},{25,1},{2,10},{10... | collective-permute-start | bytes 196616 | tf_op jit(solution)/shard_map/ppermute | solution.py:74
  126.0 92.5 %reduce-scatter.11.cloned.1.call-start = ((), (), s32[]{:S(2)}) async-start(), calls=%async_computation.9 | async-start | bytes 327680 | tf_op jit(solution)/shard_map/reduce_scatter | solution.py:104
  136.5 81.9 %copy-start = (f32[128,128]{1,0:T(8,128)S(1)}, f32[128,128]{1,0:T(8,128)}, u32[]{:S(2)}) copy-start(f32[128,128]{1,0:T(8,128)} %get-tuple-element.21) | copy-start | bytes 196612
  139.1 128.2 %reduce-scatter.13.cloned.1.call-start = ((), (), s32[]{:S(2)}) async-start(), calls=%async_computation.10 | async-start | bytes 73728 | tf_op jit(solution)/shard_map/reduce_scatter | solution.py:71
  220.8 18.4 %copy-start.6 = (f32[128,128]{1,0:T(8,128)}, f32[128,128]{1,0:T(8,128)S(1)}, u32[]{:S(2)}) copy-start(f32[128,128]{1,0:T(8,128)S(1)} %get-tuple-element.26) | copy-start | bytes 196612
  220.8 6.2 %collective-permute-start.3 = (f32[128,128]{1,0:T(8,128)S(1)}, f32[128,128]{1,0:T(8,128)S(1)}, u32[]{:S(2)}, u32[]{:S(2)}) collective-permute-start(f32[128,128]{1,0:T(8,128)S(1)} %get-tuple-element.26), channel_id=1, source_target_pairs={{0,8},{8,16},{16,24},{24,0},{1,9},{9,17},{17,25},{25,1},{2,10},{10... | collective-permute-start | bytes 196616 | tf_op jit(solution)/shard_map/ppermute | solution.py:74
  226.9 6.1 %collective-permute-start.4 = (f32[128,128]{1,0:T(8,128)S(1)}, f32[128,128]{1,0:T(8,128)S(1)}, u32[]{:S(2)}, u32[]{:S(2)}) collective-permute-start(f32[128,128]{1,0:T(8,128)S(1)} %collective-permute-done.3), channel_id=1, source_target_pairs={{0,8},{8,16},{16,24},{24,0},{1,9},{9,17},{17,25},{25,1},{2,10},{10... | collective-permute-start | bytes 196616 | tf_op jit(solution)/shard_map/ppermute | solution.py:74
  233.0 6.2 %collective-permute-start.5 = (f32[128,128]{1,0:T(8,128)S(1)}, f32[128,128]{1,0:T(8,128)}, u32[]{:S(2)}, u32[]{:S(2)}) collective-permute-start(f32[128,128]{1,0:T(8,128)S(1)} %collective-permute-done.4), channel_id=1, source_target_pairs={{0,8},{8,16},{16,24},{24,0},{1,9},{9,17},{17,25},{25,1},{2,10},{10... | collective-permute-start | bytes 196616 | tf_op jit(solution)/shard_map/ppermute | solution.py:74
  233.1 90.3 %reduce-scatter.15.cloned.1.call-start = ((), (), s32[]{:S(2)}) async-start(), calls=%async_computation.11 | async-start | bytes 327680 | tf_op jit(solution)/shard_map/reduce_scatter | solution.py:104
  244.5 78.9 %copy-start.1 = (f32[128,128]{1,0:T(8,128)S(1)}, f32[128,128]{1,0:T(8,128)}, u32[]{:S(2)}) copy-start(f32[128,128]{1,0:T(8,128)} %reduce-scatter.11.cloned.1.call-done) | copy-start | bytes 196612
  244.5 78.9 %copy-start.2 = (f32[128,128]{1,0:T(8,128)S(1)}, f32[128,128]{1,0:T(8,128)}, u32[]{:S(2)}) copy-start(f32[128,128]{1,0:T(8,128)} %get-tuple-element.23) | copy-start | bytes 196612
  247.1 124.6 %reduce-scatter.17.cloned.1.call-start = ((), (), s32[]{:S(2)}) async-start(), calls=%async_computation.12 | async-start | bytes 73728 | tf_op jit(solution)/shard_map/reduce_scatter | solution.py:71
  268.8 54.7 %copy-start.4 = (f32[16,128]{1,0:T(8,128)}, f32[16,128]{1,0:T(8,128)S(1)}, u32[]{:S(2)}) copy-start(f32[16,128]{1,0:T(8,128)S(1)} %get-tuple-element.13) | copy-start | bytes 24580
  325.1 6.2 %collective-permute-start.6 = (f32[128,128]{1,0:T(8,128)S(1)}, f32[128,128]{1,0:T(8,128)S(1)}, u32[]{:S(2)}, u32[]{:S(2)}) collective-permute-start(f32[128,128]{1,0:T(8,128)S(1)} %get-tuple-element.29), channel_id=1, source_target_pairs={{0,8},{8,16},{16,24},{24,0},{1,9},{9,17},{17,25},{25,1},{2,10},{10... | collective-permute-start | bytes 196616 | tf_op jit(solution)/shard_map/ppermute | solution.py:74
  331.3 6.1 %collective-permute-start.7 = (f32[128,128]{1,0:T(8,128)S(1)}, f32[128,128]{1,0:T(8,128)S(1)}, u32[]{:S(2)}, u32[]{:S(2)}) collective-permute-start(f32[128,128]{1,0:T(8,128)S(1)} %collective-permute-done.6), channel_id=1, source_target_pairs={{0,8},{8,16},{16,24},{24,0},{1,9},{9,17},{17,25},{25,1},{2,10},{10... | collective-permute-start | bytes 196616 | tf_op jit(solution)/shard_map/ppermute | solution.py:74
  337.4 6.1 %collective-permute-start.8 = (f32[128,128]{1,0:T(8,128)S(1)}, f32[128,128]{1,0:T(8,128)S(1)}, u32[]{:S(2)}, u32[]{:S(2)}) collective-permute-start(f32[128,128]{1,0:T(8,128)S(1)} %collective-permute-done.7), channel_id=1, source_target_pairs={{0,8},{8,16},{16,24},{24,0},{1,9},{9,17},{17,25},{25,1},{2,10},{10... | collective-permute-start | bytes 196616 | tf_op jit(solution)/shard_map/ppermute | solution.py:74
  337.5 10.6 %copy-start.11 = (f32[128]{0:T(128)S(1)}, f32[128]{0:T(128)}, u32[]{:S(2)}) copy-start(f32[128]{0:T(128)} %param.12) | copy-start | bytes 1540
  337.5 34.2 %copy-start.3 = (f32[16,128]{1,0:T(8,128)S(1)}, f32[16,128]{1,0:T(8,128)}, u32[]{:S(2)}) copy-start(f32[16,128]{1,0:T(8,128)} %reduce-scatter.13.cloned.1.call-done) | copy-start | bytes 24580
  337.5 34.2 %copy-start.5 = (f32[16,128]{1,0:T(8,128)S(1)}, f32[16,128]{1,0:T(8,128)}, u32[]{:S(2)}) copy-start(f32[16,128]{1,0:T(8,128)} %copy-done.4) | copy-start | bytes 24580
  337.5 34.1 %copy-start.9 = (s32[16]{0:T(128)S(1)}, s32[16]{0:T(128)}, u32[]{:S(2)}) copy-start(s32[16]{0:T(128)} %copy-done.8) | copy-start | bytes 196
  337.5 82.0 %all-gather.2.cloned.1.call-start = ((), (), s32[]{:S(2)}) async-start(), calls=%async_computation.13 | async-start | bytes 2621440 | tf_op jit(solution)/shard_map/all_gather | solution.py:112
Sparse Core Ops, SparseCore 0:
  62.8 23.8 reduce-scatter.6
  126.1 34.8 reduce-scatter.8
  163.9 19.9 reduce-scatter.10
  233.2 34.0 reduce-scatter.12
  269.9 19.9 reduce-scatter.14
  337.6 34.0 reduce-scatter.16
  373.8 45.6 all-gather.1
